TPU v7x, 256 devices: a whole 4x4x8 slice. The times are simulated.
256 devices in a mesh: blk: 32 (over z, y_lo, core), chan: 8 (over y_hi, x).
Axes of the slice: x: 4, y: 4 (y_hi: 2, y_lo: 2; y = y_hi * 2 + y_lo), z: 8, core: 2. Of those that a mesh axis runs over, the one named last changes fastest.
Arguments:
- spec_in: bfloat16 [256, 2, 512, 128], P('chan', None, 'blk'), may hold values from -6 to 6
- weight: bfloat16 [128, 2, 256, 256], P('blk', None, 'chan'), may hold values from -0.5 to 0.5
- pattern: int32 [128, 4, 4], P('blk'), may hold values 0 or 1
- cotangent: bfloat16 [256, 2, 512, 128], P('chan', None, 'blk'), may hold values from -6 to 6
Outputs:
- spec_out: bfloat16 [256, 2, 512, 128], P('chan', None, 'blk')
- grad_in: bfloat16 [256, 2, 512, 128], P('chan', None, 'blk')
- grad_weight: float32 [128, 2, 256, 256], P('blk', None, 'chan')
All inputs are finite; a program needn't handle non-finite values. No bound on the sum of `pattern` on one device may be relied on, other than what follows from the above.
Results may differ from a plain program's by a relative error of at most 0.001.
Values may be sent and summed in bfloat16 or wider, within the bound.
A program may use at most 128 MiB of HBM per device.

v0:
```python
import jax
import jax.numpy as jnp
from jax import lax
from jax.sharding import PartitionSpec as P


def mix_forward(x_real, x_imag, w_real, w_imag):
    form = "ism,mio->osm"
    real_part = jnp.einsum(form, x_real, w_real, preferred_element_type=jnp.float32) - jnp.einsum(
        form, x_imag, w_imag, preferred_element_type=jnp.float32
    )
    imag_part = jnp.einsum(form, x_real, w_imag, preferred_element_type=jnp.float32) + jnp.einsum(
        form, x_imag, w_real, preferred_element_type=jnp.float32
    )
    return jnp.stack([real_part, imag_part], axis=1)


def mix_input_grad(g_real, g_imag, w_real, w_imag):
    form = "osm,mio->ism"
    real_part = jnp.einsum(form, g_real, w_real, preferred_element_type=jnp.float32) + jnp.einsum(
        form, g_imag, w_imag, preferred_element_type=jnp.float32
    )
    imag_part = jnp.einsum(form, g_imag, w_real, preferred_element_type=jnp.float32) - jnp.einsum(
        form, g_real, w_imag, preferred_element_type=jnp.float32
    )
    return jnp.stack([real_part, imag_part], axis=1)


def mix_weight_grad(x_real, x_imag, g_real, g_imag):
    form = "ism,osm->mio"
    real_part = jnp.einsum(form, x_real, g_real, preferred_element_type=jnp.float32) + jnp.einsum(
        form, x_imag, g_imag, preferred_element_type=jnp.float32
    )
    imag_part = jnp.einsum(form, x_real, g_imag, preferred_element_type=jnp.float32) - jnp.einsum(
        form, x_imag, g_real, preferred_element_type=jnp.float32
    )
    return jnp.stack([real_part, imag_part], axis=1)


def local(spec_in, weight, pattern, cotangent):
    in_rows = spec_in.shape[0]
    width = weight.shape[3]
    block_size = width // pattern.shape[2]
    full_mask = jnp.repeat(
        jnp.repeat(pattern.astype(jnp.bfloat16), block_size, axis=1), block_size, axis=2
    )
    own_mask = lax.dynamic_slice_in_dim(full_mask, lax.axis_index("chan") * in_rows, in_rows, 1)
    masked = weight * own_mask[:, None]
    full_weight = lax.all_gather(masked, "blk", axis=0, tiled=True)
    x_real = spec_in[:, 0]
    x_imag = spec_in[:, 1]
    grad_full = lax.all_gather(cotangent, "chan", axis=0, tiled=True)
    w_real = full_weight[:, 0]
    w_imag = full_weight[:, 1]
    summed = lax.psum_scatter(
        mix_forward(x_real, x_imag, w_real, w_imag), "chan", scatter_dimension=0, tiled=True
    )
    spec_out = summed.astype(jnp.bfloat16)
    grad_in = mix_input_grad(grad_full[:, 0], grad_full[:, 1], w_real, w_imag).astype(jnp.bfloat16)
    gs_real = grad_full[:, 0]
    gs_imag = grad_full[:, 1]
    weight_sum = lax.psum_scatter(
        mix_weight_grad(x_real, x_imag, gs_real, gs_imag), "blk", scatter_dimension=0, tiled=True
    )
    grad_weight = weight_sum * own_mask[:, None].astype(jnp.float32)
    return (spec_out, grad_in, grad_weight)


def solution(mesh):
    in_specs = (
        P("chan", None, "blk", None),
        P("blk", None, "chan", None),
        P("blk", None, None),
        P("chan", None, "blk", None),
    )
    out_specs = (
        P("chan", None, "blk", None),
        P("chan", None, "blk", None),
        P("blk", None, "chan", None),
    )
    return jax.shard_map(local, mesh=mesh, in_specs=in_specs, out_specs=out_specs, check_vma=False)
```

profile of v0, /device:TPU:2, one launch (start us, length us, event | category | flops | bytes accessed | tf_op | source)
XLA Modules:
  0.0 498.5 jit_solution(17210475181012896570)
XLA Ops:
  7.9 0.7 convert_element_type.11
  9.3 1.6 copy_multiply_fusion
  10.9 1.0 fusion.27
  12.9 60.5 %all-gather.5.cloned.1.call-done = bf16[256,2,16,128]{3,2,1,0:T(8,128)(2,1)} async-done(((bf16[32,2,16,128]{3,2,1,0:T(8,128)(2,1)}), bf16[256,2,16,128]{3,2,1,0:T(8,128)(2,1)}) %all-gather.5.cloned.1.call-update) | async-done | bytes 2097168 | tf_op jit(solution)/shard_map/all_gather | solution.py:52
  73.4 2.9 fusion.26
  76.3 1.3 copy.52
  77.5 2.2 copy.53
  79.7 0.8 fusion.14
  80.5 0.8 add_bitcast_fusion
  81.3 0.8 fusion.8
  82.1 0.8 subtract_bitcast_fusion
  82.9 4.1 pad_maximum_fusion
  87.3 54.5 %all-gather.3.cloned.1.call-done = bf16[128,2,32,256]{3,2,0,1:T(8,128)(2,1)} async-done(((bf16[4,2,32,256]{3,2,0,1:T(8,128)(2,1)}), bf16[128,2,32,256]{3,2,0,1:T(8,128)(2,1)}) %all-gather.3.cloned.1.call-update) | async-done | bytes 4194320 | tf_op jit(solution)/shard_map/all_gather | solution.py:49
  141.8 2.2 fusion.2
  146.1 2.4 pad_maximum_fusion.1
  148.5 5.8 %copy.41 = f32[256,2,16,128]{3,2,1,0:T(8,128)} copy(f32[256,2,16,128]{0,2,3,1:T(8,128)} %pad_maximum_fusion.1) | data formatting | bytes 8388608 | tf_op jit(solution)/shard_map/stack | solution.py:15
  156.2 2.4 fusion.1
  160.2 2.4 fusion
  164.4 0.7 pad_maximum_fusion.2
  165.1 231.4 %all-reduce.3.cloned.1.call-done = f32[128,2,32,256]{3,2,0,1:T(8,128)} async-done(((f32[128,2,32,256]{3,2,0,1:T(8,128)}), f32[128,2,32,256]{3,2,0,1:T(8,128)}) %all-reduce.3.cloned.1.call-update) | async-done | bytes 8388624
  396.5 1.0 dynamic-slice_multiply_fusion
  397.4 0.7 copy.46
  398.2 92.0 %reduce-scatter.5.cloned.1.call-done = f32[32,2,16,128]{3,2,1,0:T(8,128)} async-done(((f32[256,2,16,128]{3,2,1,0:T(8,128)}), f32[32,2,16,128]{3,2,1,0:T(8,128)}) %reduce-scatter.5.cloned.1.call-update) | async-done | bytes 524304 | tf_op jit(solution)/shard_map/reduce_scatter | solution.py:55
  490.2 1.8 convert_element_type.12
  (33 shorter events, 9.2 us)
Async XLA Ops:
  7.2 66.2 %all-gather.5.cloned.1.call-start = ((), (), s32[]{:S(2)}) async-start(), calls=%async_computation.3 | async-start | bytes 2359296 | tf_op jit(solution)/shard_map/all_gather | solution.py:52
  7.9 133.9 %all-gather.3.cloned.1.call-start = ((), (), s32[]{:S(2)}) async-start(), calls=%async_computation.1 | async-start | bytes 4325376 | tf_op jit(solution)/shard_map/all_gather | solution.py:49
  10.9 385.6 %all-reduce.3.cloned.1.call-start = ((), (), s32[]{:S(2)}) async-start(), calls=%async_computation.4 | async-start | bytes 16777216
  87.1 403.1 %reduce-scatter.5.cloned.1.call-start = ((), (), s32[]{:S(2)}) async-start(), calls=%async_computation.2 | async-start | bytes 4718592 | tf_op jit(solution)/shard_map/reduce_scatter | solution.py:55
  141.8 2.8 copy-start
  154.3 0.7 copy-start.3
  156.2 2.8 copy-start.1
  160.2 2.9 copy-start.2
Sparse Core Ops, SparseCore 0:
  10.6 62.7 all-gather.4
  75.8 65.9 all-gather.2
  144.5 251.9 all-reduce.2
  400.5 89.6 reduce-scatter.4
where the time goes:
time: 499 us; the launch traced here: 498 us
  waiting for transfers between devices  439 us (88%)
  local copies, waits for them, and re-layouts  19.2 us (4%)
  between operations  14.6 us (3%)
  matrix products  13 us (3%)
  other arithmetic  12.3 us (2%)
    unnamed x5, waiting for transfers between devices  232 us
    reduce_scatter x1, waiting for transfers between devices, local(): lax.psum_scatter(mix_forward(x_real, x_imag, w_real, w_imag), 'chan', sca...  92 us
    all_gather x1, waiting for transfers between devices, local(): grad_full = lax.all_gather(cotangent, 'chan', axis=0, tiled=True)  60.5 us
    all_gather x1, waiting for transfers between devices, local(): full_weight = lax.all_gather(masked, 'blk', axis=0, tiled=True)  54.5 us
  transfers between devices with their start and end apart: 4, of which 4 were waited for; matrix products, arithmetic and copies ran while one was open for 8% of the time, Pallas kernels for 0%

commit v1 on v0

--- a/solution.py
+++ b/solution.py
@@ -2,6 +2,11 @@
 import jax.numpy as jnp
 from jax import lax
 from jax.sharding import PartitionSpec as P
+from jax.lax import all_to_all, psum
+
+chains_make = lambda mine_x, mesh_ax, array_axis: jnp.concatenate(
+    all_to_all(jnp.stack([mine_x] * psum(1, mesh_ax), 0), mesh_ax, 0, 0), array_axis
+)
 
 
 def mix_forward(x_real, x_imag, w_real, w_imag):
@@ -49,7 +54,7 @@
     full_weight = lax.all_gather(masked, "blk", axis=0, tiled=True)
     x_real = spec_in[:, 0]
     x_imag = spec_in[:, 1]
-    grad_full = lax.all_gather(cotangent, "chan", axis=0, tiled=True)
+    grad_full = chains_make(cotangent, "chan", 0)
     w_real = full_weight[:, 0]
     w_imag = full_weight[:, 1]
     summed = lax.psum_scatter(

time: 499 us -> 451 us (0.904)
  waiting for transfers between devices: 439 us -> 382 us
  starting transfers between devices: 0.34 us -> 7.72 us
    all_gather x1 -> x0, waiting for transfers between devices: 60.5 us -> none  [local(): grad_full = lax.all_gather(cotangent, 'chan', axis=0, tiled=True)]
    all_to_all x0 -> x1, waiting for transfers between devices: none -> 26.3 us  [all_to_all(jnp.stack([mine_x] * psum(1, mesh_ax), 0), mesh_ax, 0, 0)]
    all_gather x1, waiting for transfers between devices: 54.5 us -> 32.9 us  [local(): full_weight = lax.all_gather(masked, 'blk', axis=0, tiled=True)]
    all_to_all x0 -> x1, starting transfers between devices: none -> 7.46 us  [all_to_all(jnp.stack([mine_x] * psum(1, mesh_ax), 0), mesh_ax, 0, 0)]
    unnamed x5 -> x4, waiting for transfers between devices: 232 us -> 231 us
  transfers between devices with their start and end apart: 4 -> 4, of which waited for: 4 -> 4; matrix products, arithmetic and copies ran while one was open for 8% -> 9% of each run, Pallas kernels for 0% -> 0%
where the time goes in v1:
time: 451 us; the launch traced here: 450 us
  waiting for transfers between devices  382 us (85%)
  local copies, waits for them, and re-layouts  20.6 us (5%)
  between operations  14.6 us (3%)
  matrix products  13 us (3%)
  other arithmetic  12.3 us (3%)
  starting transfers between devices  7.72 us (2%)
    unnamed x4, waiting for transfers between devices  231 us
    reduce_scatter x1, waiting for transfers between devices, local(): lax.psum_scatter(mix_forward(x_real, x_imag, w_real, w_imag), 'chan', sca...  92.1 us
    all_gather x1, waiting for transfers between devices, local(): full_weight = lax.all_gather(masked, 'blk', axis=0, tiled=True)  32.9 us
    all_to_all x1, waiting for transfers between devices, all_to_all(jnp.stack([mine_x] * psum(1, mesh_ax), 0), mesh_ax, 0, 0)  26.3 us
  transfers between devices with their start and end apart: 4, of which 4 were waited for; matrix products, arithmetic and copies ran while one was open for 9% of the time, Pallas kernels for 0%

profile of v1, /device:TPU:2, one launch (start us, length us, event | category | flops | bytes accessed | tf_op | source)
XLA Modules:
  0.0 450.2 jit_solution(7479486170120768969)
XLA Ops:
  8.5 1.6 copy_multiply_fusion
  10.1 2.6 stack.44
  12.8 7.5 %all-to-all-start = ((bf16[8,32,2,16,128]{4,3,2,1,0:T(8,128)(2,1)}), bf16[8,32,2,16,128]{4,3,2,1,0:T(8,128)(2,1)S(1)}, u32[]{:S(2)}, u32[]{:S(2)}) async-start(bf16[8,32,2,16,128]{4,3,2,1,0:T(8,128)(2,1)} %stack.44), calls=%async_computation.1 | async-start | bytes 4194304 | tf_op jit(solution)/shard_map/all_to_all | solution.py:8
  21.2 26.3 %all-to-all-done = bf16[8,32,2,16,128]{4,3,2,1,0:T(8,128)(2,1)S(1)} async-done(((bf16[8,32,2,16,128]{4,3,2,1,0:T(8,128)(2,1)}), bf16[8,32,2,16,128]{4,3,2,1,0:T(8,128)(2,1)S(1)}, u32[]{:S(2)}, u32[]{:S(2)}) %all-to-all-start) | async-done | bytes 2097184 | tf_op jit(solution)/shard_map/all_to_all | solution.py:8
  47.6 1.7 fusion.26
  49.3 2.2 copy.53
  51.5 2.2 copy.54
  53.7 0.8 fusion.14
  54.5 0.8 add_bitcast_fusion
  55.3 0.8 fusion.8
  56.1 0.8 subtract_bitcast_fusion
  56.9 4.1 pad_maximum_fusion
  61.3 32.9 %all-gather.2.cloned.1.call-done = bf16[128,2,32,256]{3,2,0,1:T(8,128)(2,1)} async-done(((bf16[4,2,32,256]{3,2,0,1:T(8,128)(2,1)}), bf16[128,2,32,256]{3,2,0,1:T(8,128)(2,1)}) %all-gather.2.cloned.1.call-update) | async-done | bytes 4194320 | tf_op jit(solution)/shard_map/all_gather | solution.py:54
  94.2 2.2 fusion.2
  98.5 2.4 pad_maximum_fusion.1
  100.9 5.8 %copy.42 = f32[256,2,16,128]{3,2,1,0:T(8,128)} copy(f32[256,2,16,128]{0,2,3,1:T(8,128)} %pad_maximum_fusion.1) | data formatting | bytes 8388608 | tf_op jit(solution)/shard_map/stack | solution.py:20
  108.6 2.4 fusion.1
  112.6 2.4 fusion
  116.8 0.7 pad_maximum_fusion.2
  117.5 230.5 %all-reduce.3.cloned.1.call-done = f32[128,2,32,256]{3,2,0,1:T(8,128)} async-done(((f32[128,2,32,256]{3,2,0,1:T(8,128)}), f32[128,2,32,256]{3,2,0,1:T(8,128)}) %all-reduce.3.cloned.1.call-update) | async-done | bytes 8388624
  348.0 1.0 dynamic-slice_multiply_fusion
  349.0 0.7 copy.47
  349.7 92.1 %reduce-scatter.5.cloned.1.call-done = f32[32,2,16,128]{3,2,1,0:T(8,128)} async-done(((f32[256,2,16,128]{3,2,1,0:T(8,128)}), f32[32,2,16,128]{3,2,1,0:T(8,128)}) %reduce-scatter.5.cloned.1.call-update) | async-done | bytes 524304 | tf_op jit(solution)/shard_map/reduce_scatter | solution.py:60
  441.9 1.8 convert_element_type.12
  (35 shorter events, 9.2 us)
Async XLA Ops:
  7.2 87.0 %all-gather.2.cloned.1.call-start = ((), (), s32[]{:S(2)}) async-start(), calls=%async_computation.2 | async-start | bytes 4325376 | tf_op jit(solution)/shard_map/all_gather | solution.py:54
  8.2 12.0 %copy-start.3 = (bf16[32,2,16,128]{3,2,1,0:T(8,128)(2,1)S(1)}, bf16[32,2,16,128]{3,2,1,0:T(8,128)(2,1)}, u32[]{:S(2)}) copy-start(bf16[32,2,16,128]{3,2,1,0:T(8,128)(2,1)} %param.4) | copy-start | bytes 786436
  12.8 34.8 %all-to-all-start = ((bf16[8,32,2,16,128]{4,3,2,1,0:T(8,128)(2,1)}), bf16[8,32,2,16,128]{4,3,2,1,0:T(8,128)(2,1)S(1)}, u32[]{:S(2)}, u32[]{:S(2)}) async-start(bf16[8,32,2,16,128]{4,3,2,1,0:T(8,128)(2,1)} %stack.44), calls=%async_computation.1 | async-start | bytes 4194304 | tf_op jit(solution)/shard_map/all_to_all | solution.py:8
  20.2 327.8 %all-reduce.3.cloned.1.call-start = ((), (), s32[]{:S(2)}) async-start(), calls=%async_computation.4 | async-start | bytes 16777216
  61.0 380.8 %reduce-scatter.5.cloned.1.call-start = ((), (), s32[]{:S(2)}) async-start(), calls=%async_computation.3 | async-start | bytes 4718592 | tf_op jit(solution)/shard_map/reduce_scatter | solution.py:60
  94.2 2.8 copy-start
  106.7 0.7 copy-start.4
  108.6 2.8 copy-start.1
  112.6 2.9 copy-start.2
Sparse Core Ops, SparseCore 0:
  10.4 83.7 all-gather.1
  96.9 251.1 all-reduce.2
  352.2 89.6 reduce-scatter.4
